TPU v7x, 32 devices: a whole 2x2x4 slice. The times are simulated.
32 devices in a mesh: dir: 2 (over y), dp: 16 (over z, x, core).
Axes of the slice: x: 2, y: 2, z: 4, core: 2. Of those that a mesh axis runs over, the one named last changes fastest.
Arguments:
- tokens: bfloat16 [16, 1024, 768], P('dp', 'dir'), may hold values from -6 to 6
- norm_gain: float32 [768], replicated, may hold values from 0.5 to 1.5
- w_zx: bfloat16 [768, 3072], P('dp'), may hold values from -0.21875 to 0.21875
- w_bc: bfloat16 [768, 128], P('dp'), may hold values from -0.21875 to 0.21875
- w_dt: bfloat16 [768, 48], P('dp'), may hold values from -0.21875 to 0.21875
- conv_w: float32 [4, 1664], replicated, may hold values from -3 to 3
- conv_b: float32 [1664], replicated, may hold values from -1.75 to 1.75
- dt_bias: float32 [48], replicated, may hold values from -4.5 to -2
- a_log: float32 [48], replicated, may hold values from -2.5 to 1.5
- d_skip: float32 [24], replicated, may hold values from 0.5 to 1.5
- out_gain: float32 [1536], replicated, may hold values from 0.5 to 1.5
- w_out: bfloat16 [1536, 768], P('dp'), may hold values from -0.15625 to 0.15625
- doc_lengths: int32 [16, 4], P('dp'), may hold values from 1 to 512, 1024 in all within a row
- out_grad: bfloat16 [16, 1024, 768], P('dp', 'dir'), may hold values from -6 to 6
Outputs:
- block_out: bfloat16 [16, 1024, 768], P('dp', 'dir')
- grad_tokens: bfloat16 [16, 1024, 768], P('dp', 'dir')
- grad_norm_gain: float32 [768], replicated
- grad_w_zx: float32 [768, 3072], replicated
- grad_w_bc: float32 [768, 128], replicated
- grad_w_dt: float32 [768, 48], replicated
- grad_conv_w: float32 [4, 1664], replicated
- grad_conv_b: float32 [1664], replicated
- grad_dt_bias: float32 [48], replicated
- grad_a_log: float32 [48], replicated
- grad_d_skip: float32 [24], replicated
- grad_out_gain: float32 [1536], replicated
- grad_w_out: float32 [1536, 768], replicated
Inputs may be any that keep to these rules, and one draw needn't show every extreme that they name: `doc_lengths`: in each row the 4 lengths sum to 1024, and the longest is exactly 512.
All inputs are finite; a program needn't handle non-finite values.
Results may differ from a plain program's by a relative error of at most 0.014.
Values may be sent and summed in bfloat16 or wider, within the bound.
No kernel may reach another device: no remote copies, remote signals or barrier semaphores. Data moves between devices by JAX's collectives and lax.ppermute only.
A program may use at most 192 MiB of HBM per device.

v0:
```python
from functools import partial
import jax
import jax.numpy as jnp
from jax import lax
from jax.sharding import PartitionSpec as P

D = 768
HEADS = 24
HEADDIM = 64
STATE = 64
INNER = 1536
BLOCK = 128
CONV = 4
LEN = 1024
highest = lax.Precision.HIGHEST
epsilon = 1e-05


def shifted_2(block, axis, distance):
    devices = range(lax.axis_size(axis))
    route = [(i - distance, i) for i in devices if i - distance in devices]
    return lax.ppermute(block, axis, route)


def partner(shard, axis, stride):
    return lax.ppermute(shard, axis, [(i, i ^ 1 << stride) for i in range(lax.axis_size(axis))])


def segment_ids(lengths_row, length):
    doc_ends = jnp.cumsum(lengths_row)
    places = jnp.arange(length, dtype=jnp.int32)
    return jnp.sum((places[:, None] >= doc_ends[None, :]).astype(jnp.int32), axis=1)


def conv_silu(pre_conv, seg_row, conv_w, conv_b):
    tap_count = conv_w.shape[0]
    row_len = pre_conv.shape[0]
    padded = jnp.pad(pre_conv, ((tap_count - 1, 0), (0, 0)))
    seg_pad = jnp.concatenate([jnp.full((tap_count - 1,), -1, jnp.int32), seg_row], axis=0)
    summed = conv_b[None, :] + conv_w[tap_count - 1][None, :] * pre_conv
    for offset in range(1, tap_count):
        start = tap_count - 1 - offset
        shifted = padded[start : start + row_len]
        same_doc = (seg_pad[start : start + row_len] == seg_row)[:, None]
        summed = summed + jnp.where(
            same_doc, conv_w[tap_count - 1 - offset][None, :] * shifted, 0.0
        )
    return jax.nn.silu(summed)


def block_step(a_neg, carried, inputs):
    states, prev_seg = carried
    x_block, b_block, c_block, dt_block, seg_block = inputs
    block_len = x_block.shape[0]
    log_rates = dt_block * a_neg[None, :]
    cumul = jnp.cumsum(log_rates, axis=0)
    cum_heads = cumul.T
    places = jnp.arange(block_len, dtype=jnp.int32)
    keep_mask = (places[:, None] > places[None, :]) & (seg_block[:, None] == seg_block[None, :])
    scores = jnp.dot(c_block, b_block.T, precision=highest)
    weighted = jnp.where(
        keep_mask[None],
        jnp.exp(jnp.minimum(cum_heads[:, :, None] - cum_heads[:, None, :], 0.0)) * scores[None],
        0.0,
    )
    inputs_dt = x_block * dt_block[:, :, None]
    y_inner = jnp.einsum("hts,shp->thp", weighted, inputs_dt, precision=highest)
    carried_in = jnp.where((seg_block == prev_seg)[:, None], jnp.exp(cumul), 0.0)
    y_carry = jnp.einsum("tn,hpn->thp", c_block, states, precision=highest) * carried_in[:, :, None]
    last_seg = seg_block[block_len - 1]
    tail_weights = jnp.where(
        (seg_block == last_seg)[:, None], jnp.exp(cumul[block_len - 1][None, :] - cumul), 0.0
    )
    carry_keep = jnp.where(last_seg == prev_seg, jnp.exp(cumul[block_len - 1]), 0.0)
    new_states = states * carry_keep[:, None, None] + jnp.einsum(
        "shp,sn->hpn", inputs_dt * tail_weights[:, :, None], b_block, precision=highest
    )
    return ((new_states, last_seg), y_inner + y_carry)


def scan_dir(x_row, b_row, c_row, dt_row, a_neg, seg_row):
    length = x_row.shape[0]
    block_count = length // BLOCK
    head_count = dt_row.shape[1]
    head_width = x_row.shape[1] // head_count
    state_width = b_row.shape[1]
    sliced = (
        x_row.reshape(block_count, BLOCK, head_count, head_width),
        b_row.reshape(block_count, BLOCK, state_width),
        c_row.reshape(block_count, BLOCK, state_width),
        dt_row.reshape(block_count, BLOCK, head_count),
        seg_row.reshape(block_count, BLOCK),
    )
    initial = (
        jnp.zeros((head_count, head_width, state_width), x_row.dtype),
        jnp.array(-1, jnp.int32),
    )
    advance = jax.checkpoint(partial(block_step, a_neg))
    final_carry, results = lax.scan(advance, initial, sliced)
    return (results.reshape(length, head_count * head_width), final_carry[0])


def rms_scale(values, gain):
    return (
        values
        * lax.rsqrt(jnp.mean(values * values, axis=1, keepdims=True) + epsilon)
        * gain[None, :]
    )


def gate_norm(mixed_vals, gate_vals, gain):
    gated = mixed_vals * jax.nn.silu(gate_vals)
    return (
        gated * lax.rsqrt(jnp.mean(gated * gated, axis=1, keepdims=True) + epsilon) * gain[None, :]
    )


def body(
    tokens,
    norm_gain,
    w_zx,
    w_bc,
    w_dt,
    conv_w,
    conv_b,
    dt_bias,
    a_log,
    d_skip,
    out_gain,
    w_out,
    doc_lengths,
    out_grad,
):
    direction = lax.axis_index("dir")
    forward_side = direction == 0
    full_zx, full_bc, full_dt, full_out = (
        lax.all_gather(w_zx, "dp", axis=0, tiled=True),
        lax.all_gather(w_bc, "dp", axis=0, tiled=True),
        lax.all_gather(w_dt, "dp", axis=0, tiled=True),
        lax.all_gather(w_out, "dp", axis=0, tiled=True),
    )
    row_count = tokens.shape[0]
    half_len = tokens.shape[1]
    token_count = row_count * half_len
    x_flat = tokens.reshape(token_count, D).astype(jnp.float32)
    normed_f, rms_pull = jax.vjp(rms_scale, x_flat, norm_gain)
    normed = normed_f.astype(jnp.bfloat16)
    zx_proj = jnp.dot(normed, full_zx, preferred_element_type=jnp.float32)
    bc_proj = jnp.dot(normed, full_bc, preferred_element_type=jnp.float32)
    dt_proj = jnp.dot(normed, full_dt, preferred_element_type=jnp.float32).astype(jnp.bfloat16)
    gate_z = zx_proj[:, :INNER]
    pre_conv = jnp.concatenate([zx_proj[:, INNER:], bc_proj], axis=1).astype(jnp.bfloat16)
    seg_rows = jax.vmap(partial(segment_ids, length=LEN))(doc_lengths)
    pre_rows = pre_conv.reshape(row_count, half_len, INNER + 2 * STATE)
    dt_rows = dt_proj.reshape(row_count, half_len, 2 * HEADS)
    rim_len = CONV - 1
    rim_in = shifted_2(pre_rows[:, half_len - rim_len :, :], "dir", 1)
    pre_ext = jnp.concatenate([rim_in, pre_rows], axis=1).astype(jnp.float32)
    seg_padded = jnp.concatenate([jnp.full((row_count, rim_len), -1, jnp.int32), seg_rows], axis=1)
    seg_ext = lax.dynamic_slice_in_dim(seg_padded, direction * half_len, half_len + rim_len, 1)
    seam_fwd = seg_rows[:, half_len - 1]
    seam_rev = seg_rows[:, half_len]

    def local_mixer(pre_vals, dt_vals, conv_w_in, conv_b_in, bias_in, alog_in, skip_in):
        a_fwd = -jnp.exp(alog_in[:HEADS])
        a_rev = -jnp.exp(alog_in[HEADS:])
        skip_cols = jnp.repeat(skip_in, HEADDIM)

        def one_half(row_args):
            pre_row, dt_row, seg_row, fwd_seam, rev_seam = row_args
            conv_out = conv_silu(pre_row, seg_row, conv_w_in, conv_b_in)[rim_len:]
            seg_here = seg_row[rim_len:]
            dt_fwd = jax.nn.softplus(dt_row[:, :HEADS] + bias_in[None, :HEADS])
            dt_rev = jax.nn.softplus(dt_row[:, HEADS:] + bias_in[None, HEADS:])
            x_in = conv_out[:, :INNER]
            b_in = conv_out[:, INNER : INNER + STATE]
            c_in = conv_out[:, INNER + STATE :]
            y_fwd, state_fwd = scan_dir(x_in, b_in, c_in, dt_fwd, a_fwd, seg_here)
            y_flip, state_rev = scan_dir(
                jnp.flip(x_in, axis=0),
                jnp.flip(b_in, axis=0),
                jnp.flip(c_in, axis=0),
                jnp.flip(dt_rev, axis=0),
                a_rev,
                jnp.flip(seg_here, axis=0),
            )
            y_local = y_fwd + jnp.flip(y_flip, axis=0) + x_in * skip_cols[None, :]
            sending = jnp.where(forward_side, state_fwd, state_rev)
            cum_fwd = jnp.cumsum(dt_fwd * a_fwd[None, :], axis=0)
            cum_rev = jnp.flip(
                jnp.cumsum(jnp.flip(dt_rev * a_rev[None, :], axis=0), axis=0), axis=0
            )
            carry_rev = jnp.where((seg_here == rev_seam)[:, None], jnp.exp(cum_rev), 0.0)
            carry_fwd = jnp.where((seg_here == fwd_seam)[:, None], jnp.exp(cum_fwd), 0.0)
            carry_weight = jnp.where(forward_side, carry_rev, carry_fwd)
            return (y_local, sending, c_in, carry_weight)

        return lax.map(one_half, (pre_vals, dt_vals, seg_ext, seam_fwd, seam_rev))

    local_parts, local_pull = jax.vjp(
        local_mixer, pre_ext, dt_rows.astype(jnp.float32), conv_w, conv_b, dt_bias, a_log, d_skip
    )
    y_local, sending, c_kept, carry_kept = local_parts
    received = partner(sending.astype(jnp.bfloat16), "dir", 0).astype(sending.dtype)

    def seam_term(state_in, c_vals, weights):
        term = (
            jnp.einsum("rtn,rhpn->rthp", c_vals, state_in, precision=highest)
            * weights[:, :, :, None]
        )
        return term.reshape(row_count, half_len, INNER)

    correction, seam_pull = jax.vjp(seam_term, received, c_kept, carry_kept)
    mixed = y_local + correction
    mixed_flat = mixed.reshape(token_count, INNER)
    normed_out_f, gate_pull = jax.vjp(gate_norm, mixed_flat, gate_z, out_gain)
    normed_out = normed_out_f.astype(jnp.bfloat16)
    summed_out = x_flat + jnp.dot(normed_out, full_out, preferred_element_type=jnp.float32)
    block_out = summed_out.astype(jnp.bfloat16).reshape(row_count, half_len, D)
    grad_flat = out_grad.reshape(token_count, D)
    grad_w_out = jnp.einsum("tk,td->kd", normed_out, grad_flat, preferred_element_type=jnp.float32)
    grad_normed_out = jnp.einsum(
        "td,kd->tk", grad_flat, full_out, preferred_element_type=jnp.float32
    )
    grad_mixed, grad_gate, grad_out_gain = gate_pull(grad_normed_out)
    grad_mixed_low = grad_mixed.astype(jnp.bfloat16).reshape(row_count, half_len, INNER)
    grad_mixed_vals = grad_mixed_low.astype(jnp.float32)
    grad_received, grad_c_seam, grad_carry = seam_pull(grad_mixed_vals)
    grad_sending = partner(grad_received.astype(jnp.bfloat16), "dir", 0).astype(grad_received.dtype)
    grad_ext, grad_dt_half, grad_conv_w, grad_conv_b, grad_dt_bias, grad_a_log, grad_d_skip = (
        local_pull((grad_mixed_vals, grad_sending, grad_c_seam, grad_carry))
    )
    rim_back = shifted_2(grad_ext[:, :rim_len, :], "dir", -1)
    grad_pre_half = grad_ext[:, rim_len:, :] + jnp.pad(
        rim_back, ((0, 0), (half_len - rim_len, 0), (0, 0))
    )
    grad_pre_flat = grad_pre_half.reshape(token_count, INNER + 2 * STATE)
    grad_zx = jnp.concatenate([grad_gate, grad_pre_flat[:, :INNER]], axis=1).astype(jnp.bfloat16)
    grad_bc = grad_pre_flat[:, INNER:].astype(jnp.bfloat16)
    grad_dt_low = grad_dt_half.reshape(token_count, 2 * HEADS).astype(jnp.bfloat16)
    grad_w_zx = jnp.einsum("tk,tj->kj", normed, grad_zx, preferred_element_type=jnp.float32)
    grad_w_bc = jnp.einsum("tk,tj->kj", normed, grad_bc, preferred_element_type=jnp.float32)
    grad_w_dt = jnp.einsum("tk,tj->kj", normed, grad_dt_low, preferred_element_type=jnp.float32)
    grad_normed = (
        jnp.einsum("tj,kj->tk", grad_zx, full_zx, preferred_element_type=jnp.float32)
        + jnp.einsum("tj,kj->tk", grad_bc, full_bc, preferred_element_type=jnp.float32)
        + jnp.einsum("tj,kj->tk", grad_dt_low, full_dt, preferred_element_type=jnp.float32)
    )
    grad_x_norm, grad_norm_gain = rms_pull(grad_normed)
    grad_tokens = (
        (grad_flat.astype(jnp.float32) + grad_x_norm)
        .astype(jnp.bfloat16)
        .reshape(row_count, half_len, D)
    )
    (
        sum_norm_gain,
        sum_w_zx,
        sum_w_bc,
        sum_w_dt,
        sum_conv_w,
        sum_conv_b,
        sum_dt_bias,
        sum_a_log,
        sum_d_skip,
        sum_out_gain,
        sum_w_out,
    ) = lax.psum(
        (
            grad_norm_gain,
            grad_w_zx,
            grad_w_bc,
            grad_w_dt,
            grad_conv_w,
            grad_conv_b,
            grad_dt_bias,
            grad_a_log,
            grad_d_skip,
            grad_out_gain,
            grad_w_out,
        ),
        ("dir", "dp"),
    )
    return (
        block_out,
        grad_tokens,
        sum_norm_gain,
        sum_w_zx,
        sum_w_bc,
        sum_w_dt,
        sum_conv_w,
        sum_conv_b,
        sum_dt_bias,
        sum_a_log,
        sum_d_skip,
        sum_out_gain,
        sum_w_out,
    )


def solution(mesh):
    placed = (
        P("dp", "dir", None),
        P(),
        P("dp", None),
        P("dp", None),
        P("dp", None),
        P(),
        P(),
        P(),
        P(),
        P(),
        P(),
        P("dp", None),
        P("dp", None),
        P("dp", "dir", None),
    )
    return jax.shard_map(
        body,
        mesh=mesh,
        in_specs=placed,
        out_specs=(
            P("dp", "dir", None),
            P("dp", "dir", None),
            P(),
            P(),
            P(),
            P(),
            P(),
            P(),
            P(),
            P(),
            P(),
            P(),
            P(),
        ),
        check_vma=False,
    )
```

profile of v0, /device:TPU:0, one launch (start us, length us, event | category | flops | bytes accessed | tf_op | source)
XLA Modules:
  0.0 1082.4 jit_solution(1993637158967317221)
XLA Ops:
  10.2 24.4 %all_gather.14 = bf16[768,128]{1,0:T(8,128)(2,1)S(1)} all-gather(bf16[48,128]{1,0:T(8,128)(2,1)} %param.28), channel_id=1, replica_groups=mesh['dir'=2,'dp'=16] {'dp'}, dimensions={0}, use_global_device_ids=true | all-gather | bytes 208896 | tf_op jit(solution)/shard_map/all_gather | solution.py:138
  37.3 18.9 %all_gather.12 = bf16[768,48]{1,0:T(8,128)(2,1)S(1)} all-gather(bf16[48,48]{1,0:T(8,128)(2,1)} %param.29), channel_id=1, replica_groups=mesh['dir'=2,'dp'=16] {'dp'}, dimensions={0}, use_global_device_ids=true | all-gather | bytes 78336 | tf_op jit(solution)/shard_map/all_gather | solution.py:139
  67.4 4.6 fusion.288
  84.9 4.9 fusion.204
  93.8 24.7 %rev.107 = f32[512,1536]{1,0:T(8,128)} reverse(f32[512,1536]{1,0:T(8,128)} %slice.328), dimensions={0} | reverse | bytes 6291456 | tf_op jit(solution)/shard_map/jvp()/while/body/eval_jaxpr/jit(_flip)/rev | solution.py:180
  118.5 5.5 reshape.1386
  124.5 5.5 reshape.1387
  129.9 6.1 copy.490
  140.6 59.0 %while.230 = (s32[]{:T(128)}, f32[24,64,64]{2,1,0:T(8,128)S(1)}, s32[]{:T(128)}, f32[4,128,24,64]{1,3,2,0:T(8,128)}, f32[4,24,64,64]{3,2,1,0:T(8,128)}, /*index=...) while((s32[]{:T(128)}, f32[24,64,64]{2,1,0:T(8,128)S(1)}, ...), condition=%wide.region_8.10_spmd.clone, body=%wide.region_6.9_spmd.clone.sunk | while | flops 620061952 | bytes 7651091 | solution.py:99
  142.1 4.3 fusion.442
  156.8 4.3 fusion.442
  171.6 4.3 fusion.442
  186.3 4.3 fusion.442
  202.6 6.2 copy.484
  213.5 63.2 %while.229 = (s32[]{:T(128)}, f32[24,64,64]{2,1,0:T(8,128)S(1)}, s32[]{:T(128)}, f32[4,128,24,64]{1,3,2,0:T(8,128)}, f32[4,24,64,64]{3,2,1,0:T(8,128)}, /*index=...) while((s32[]{:T(128)}, f32[24,64,64]{2,1,0:T(8,128)S(1)}, ...), condition=%wide.region_5.7_spmd.clone, body=%wide.region_3.6_spmd.clone.sunk | while | flops 620061952 | bytes 7257875 | solution.py:99
  215.4 4.3 fusion.431
  231.0 4.3 fusion.431
  246.7 4.3 fusion.431
  262.5 4.3 fusion.431
  280.4 5.9 copy.544
  286.3 4.7 reshape.1381
  291.0 15.7 %rev.110 = f32[512,1536]{1,0:T(8,128)} reverse(f32[512,1536]{1,0:T(8,128)S(1)} %reshape.1381), dimensions={0} | reverse | bytes 6291456 | tf_op jit(solution)/shard_map/jvp()/while/body/eval_jaxpr/jit(_flip)/rev | solution.py:187
  306.7 5.9 copy.543
  312.6 6.3 reshape.1380
  318.9 5.2 broadcast_multiply_fusion.4
  327.7 7.1 multiply_reduce_fusion.16
  340.2 5.0 multiply_reduce_fusion.12
  345.7 5.7 multiply_reduce_fusion.13
  361.0 5.5 fusion.230
  371.7 5.0 reduce-window.64
  380.5 15.9 %reverse.3 = f32[512,1536]{1,0:T(8,128)} reverse(bf16[512,1536]{1,0:T(8,128)(2,1)S(1)} %get-tuple-element.2333), dimensions={0} | reverse | bytes 4718592 | tf_op jit(solution)/shard_map/reverse
  396.4 6.2 copy.519
  404.1 5.0 reduce-window.66
  413.3 6.1 copy.511
  424.7 144.4 %while.232 = (s32[]{:T(128)}, f32[24]{0:T(128)}, f32[24,64,64]{2,1,0:T(8,128)S(1)}, f32[4,128,24,64]{1,3,2,0:T(8,128)}, f32[4,128,64]{1,2,0:T(8,128)}, /*index=5...) while((s32[]{:T(128)}, f32[24]{0:T(128)}, ...), condition=%wide.region_40.42_spmd.clone, body=%wide.region_28.41_spmd.clone.sunk | while | flops 1408011520 | bytes 22274224 | solution.py:99
  438.4 4.8 multiply_reduce_fusion.28
  444.2 4.7 fusion.494
  474.4 4.8 multiply_reduce_fusion.28
  480.2 4.7 fusion.494
  510.3 4.8 multiply_reduce_fusion.28
  516.2 4.7 fusion.494
  546.3 4.8 multiply_reduce_fusion.28
  552.1 4.7 fusion.494
  574.8 142.2 %while.231 = (s32[]{:T(128)}, f32[24]{0:T(128)}, f32[24,64,64]{2,1,0:T(8,128)S(1)}, f32[4,128,24,64]{1,3,2,0:T(8,128)}, f32[4,128,64]{1,2,0:T(8,128)}, /*index=5...) while((s32[]{:T(128)}, f32[24]{0:T(128)}, ...), condition=%wide.region_27.29_spmd.clone, body=%wide.region_15.28_spmd.clone.sunk | while | flops 1408011520 | bytes 19111204 | solution.py:99
  588.5 4.5 multiply_reduce_fusion.25
  594.1 4.3 fusion.463
  624.0 4.5 multiply_reduce_fusion.25
  629.6 4.3 fusion.463
  659.5 4.5 multiply_reduce_fusion.25
  665.1 4.3 fusion.463
  695.0 4.5 multiply_reduce_fusion.25
  700.6 4.3 fusion.463
  725.9 5.8 copy.553
  731.7 6.3 reshape.1385
  738.0 4.0 copy.552
  742.0 6.2 reshape.1384
  748.2 24.7 %rev.115 = f32[512,1536]{1,0:T(8,128)} reverse(f32[512,1536]{1,0:T(8,128)} %reshape.1384), dimensions={0} | reverse | bytes 6291456 | tf_op jit(solution)/shard_map/transpose(jvp())/while/body/eval_jaxpr/jit(_flip)/rev | solution.py:180
  783.2 5.5 multiply_reduce_fusion.11
  800.1 5.6 fusion.210
  807.7 4.4 fusion.229
  814.2 5.6 fusion.221
  819.8 42.1 %all-reduce.25 = (f32[768]{0:T(1024)}, f32[4,1664]{1,0:T(4,128)}, f32[1664]{0:T(1024)}, f32[48]{0:T(128)}, f32[48]{0:T(128)}, /*index=5*/f32[24]{0:T(128)}, f32[1536]{0:T(1024)}) all-reduce(f32[768]{0:T(1024)S(1)} %get-tuple-element.2195, f32[4,1664]{1,0:T(4,128)S(1)} %pad_add_fusion.3, ...), channel_id=1, replica_groups=mesh['dir'=2,'dp'=16] {'dir','dp'}, use_global_device_ids=true, to_apply=%region_48.50 | all-reduce | flops 10744 | bytes 85952 | tf_op jit(solution)/shard_map/psum | solution.py:267
  863.3 199.8 %all-reduce.29.cloned.1.call-done = (f32[768,3072]{1,0:T(8,128)}, f32[768,128]{1,0:T(8,128)}, f32[768,48]{0,1:T(8,128)}, f32[1536,768]{1,0:T(8,128)}) async-done(((f32[768,3072]{1,0:T(8,128)}, f32[768,128]{1,0:T(8,128)}, f32[768,48]{0,1:T(8,128)}, f32[1536,768]{1,0:T(8,128)}), (f32[768,3072]{1,0:T(8,128)}, f32[768,128]{1,0:T(8,128)}, f32[768,48]{0,1:T(8,128)}, ...) | async-done | bytes 14696464 | tf_op jit(solution)/shard_map/psum | solution.py:267
  1063.1 8.8 copy.749
  (943 shorter events, 410.1 us)
Async XLA Ops:
  7.2 50.6 %copy-start.20 = (bf16[1,512,768]{2,1,0:T(8,128)(2,1)S(1)}, bf16[1,512,768]{2,1,0:T(8,128)(2,1)}, u32[]{:S(2)}) copy-start(bf16[1,512,768]{2,1,0:T(8,128)(2,1)} %param.25) | copy-start | bytes 2359300
  7.2 50.6 %copy-start.65 = (f32[768]{0:T(1024)S(1)}, f32[768]{0:T(1024)}, u32[]{:S(2)}) copy-start(f32[768]{0:T(1024)} %param.26) | copy-start | bytes 9220
  7.2 51.2 %copy-start.120 = (f32[48]{0:T(128)S(1)}, f32[48]{0:T(128)}, u32[]{:S(2)}) copy-start(f32[48]{0:T(128)} %param.32) | copy-start | bytes 580
  7.2 51.2 %copy-start.112 = (f32[48]{0:T(128)S(1)}, f32[48]{0:T(128)}, u32[]{:S(2)}) copy-start(f32[48]{0:T(128)} %param.33) | copy-start | bytes 580
  7.2 60.2 %all-gather.3.cloned.1.call-start = ((), (), s32[]{:S(2)}) async-start(), calls=%async_computation | async-start | bytes 5013504 | tf_op jit(solution)/shard_map/all_gather | solution.py:137
  8.0 332.2 %all-gather.5.cloned.1.call-start = ((), (), s32[]{:S(2)}) async-start(), calls=%async_computation.1 | async-start | bytes 2506752 | tf_op jit(solution)/shard_map/all_gather | solution.py:140
  8.7 1054.4 %all-reduce.29.cloned.1.call-start = ((), (), s32[]{:S(2)}) async-start(), calls=%async_computation.2 | async-start | bytes 29392896 | tf_op jit(solution)/shard_map/psum | solution.py:267
  10.1 48.9 %copy-start.97 = (f32[512]{0:T(512)}, f32[512]{0:T(512)S(1)}, u32[]{:S(2)}) copy-start(f32[512]{0:T(512)S(1)} %fusion.222) | copy-start | bytes 6148
  10.1 61.9 %copy-start.70 = (f32[512]{0:T(512)}, f32[512]{0:T(512)S(1)}, u32[]{:S(2)}) copy-start(f32[512]{0:T(512)S(1)} %fusion.273) | copy-start | bytes 6148
  34.6 37.5 %copy-start.47 = (bf16[768,128]{1,0:T(8,128)(2,1)}, bf16[768,128]{1,0:T(8,128)(2,1)S(1)}, u32[]{:S(2)}) copy-start(bf16[768,128]{1,0:T(8,128)(2,1)S(1)} %all_gather.14) | copy-start | bytes 589828
  36.2 48.7 %copy-start.105 = (pred[515]{0:T(1024)(128)(4,1)}, pred[515]{0:T(1024)(128)(4,1)S(1)}, u32[]{:S(2)}) copy-start(pred[515]{0:T(1024)(128)(4,1)S(1)} %get-tuple-element.2392) | copy-start | bytes 1549
  36.2 48.7 %copy-start.107 = (pred[515]{0:T(1024)(128)(4,1)}, pred[515]{0:T(1024)(128)(4,1)S(1)}, u32[]{:S(2)}) copy-start(pred[515]{0:T(1024)(128)(4,1)S(1)} %get-tuple-element.2393) | copy-start | bytes 1549
  36.2 48.7 %copy-start.109 = (pred[515]{0:T(1024)(128)(4,1)}, pred[515]{0:T(1024)(128)(4,1)S(1)}, u32[]{:S(2)}) copy-start(pred[515]{0:T(1024)(128)(4,1)S(1)} %get-tuple-element.2394) | copy-start | bytes 1549
  37.2 47.7 %copy-start.80 = (f32[1664]{0:T(1024)}, f32[1664]{0:T(1024)S(1)}, u32[]{:S(2)}) copy-start(f32[1664]{0:T(1024)S(1)} %get-tuple-element.2197) | copy-start | bytes 19972
  37.2 47.7 %copy-start.82 = (f32[1664]{0:T(1024)}, f32[1664]{0:T(1024)S(1)}, u32[]{:S(2)}) copy-start(f32[1664]{0:T(1024)S(1)} %get-tuple-element.2198) | copy-start | bytes 19972
  37.2 47.7 %copy-start.84 = (f32[1664]{0:T(1024)}, f32[1664]{0:T(1024)S(1)}, u32[]{:S(2)}) copy-start(f32[1664]{0:T(1024)S(1)} %get-tuple-element.2199) | copy-start | bytes 19972
  37.2 47.7 %copy-start.86 = (f32[1664]{0:T(1024)}, f32[1664]{0:T(1024)S(1)}, u32[]{:S(2)}) copy-start(f32[1664]{0:T(1024)S(1)} %get-tuple-element.2200) | copy-start | bytes 19972
  56.2 15.8 %copy-start.49 = (bf16[768,48]{1,0:T(8,128)(2,1)}, bf16[768,48]{1,0:T(8,128)(2,1)S(1)}, u32[]{:S(2)}) copy-start(bf16[768,48]{1,0:T(8,128)(2,1)S(1)} %all_gather.12) | copy-start | bytes 221188
  57.8 25.9 %copy-start.42 = (bf16[512,128]{1,0:T(8,128)(2,1)}, bf16[512,128]{1,0:T(8,128)(2,1)S(1)}, u32[]{:S(2)}) copy-start(bf16[512,128]{1,0:T(8,128)(2,1)S(1)} %convolution_convert_fusion.1) | copy-start | bytes 393220
  59.0 13.1 %copy-start.118 = (f32[24]{0:T(128)}, f32[24]{0:T(128)S(1)}, u32[]{:S(2)}) copy-start(f32[24]{0:T(128)S(1)} %get-tuple-element.2410) | copy-start | bytes 292
  59.8 19.6 %copy-start.56 = (f32[512,24]{0,1:T(8,128)}, f32[512,24]{0,1:T(8,128)S(1)}, u32[]{:S(2)}) copy-start(f32[512,24]{0,1:T(8,128)S(1)} %get-tuple-element.2343) | copy-start | bytes 147460
  59.8 20.1 %copy-start.52 = (f32[512,24]{0,1:T(8,128)}, f32[512,24]{0,1:T(8,128)S(1)}, u32[]{:S(2)}) copy-start(f32[512,24]{0,1:T(8,128)S(1)} %get-tuple-element.2387) | copy-start | bytes 147460
  75.0 8.7 collective-permute-start
  81.6 246.0 %copy-start.78 = (f32[1536]{0:T(1024)}, f32[1536]{0:T(1024)S(1)}, u32[]{:S(2)}) copy-start(f32[1536]{0:T(1024)S(1)} %mul.1288) | copy-start | bytes 18436
  91.7 32.3 %copy-start.37 = (f32[512,64]{1,0:T(8,128)}, f32[512,64]{1,0:T(8,128)S(1)}, u32[]{:S(2)}) copy-start(f32[512,64]{1,0:T(8,128)S(1)} %get-tuple-element.2379) | copy-start | bytes 393220
  91.7 32.5 %copy-start.36 = (f32[512,64]{1,0:T(8,128)}, f32[512,64]{1,0:T(8,128)S(1)}, u32[]{:S(2)}) copy-start(f32[512,64]{1,0:T(8,128)S(1)} %get-tuple-element.2378) | copy-start | bytes 393220
  199.6 9.2 copy-start.28
  199.6 9.1 copy-start.33
  199.6 9.1 copy-start.34
  213.5 64.1 %copy-start.54 = (f32[512,24]{0,1:T(8,128)S(1)}, f32[512,24]{0,1:T(8,128)}, u32[]{:S(2)}) copy-start(f32[512,24]{0,1:T(8,128)} %rev.112) | copy-start | bytes 147460
  277.6 41.4 %collective-permute-start.1 = (bf16[1,24,64,64]{3,2,1,0:T(8,128)(2,1)}, bf16[1,24,64,64]{3,2,1,0:T(8,128)(2,1)}, u32[]{:S(2)}, u32[]{:S(2)}) collective-permute-start(bf16[1,24,64,64]{3,2,1,0:T(8,128)(2,1)} %fusion.246), channel_id=1, source_target_pairs={{0,16},{16,0},{1,17},{17,1},{2,18},{18,2},{3,19},{19,3},{4,20},{20... | collective-permute-start | bytes 589832 | tf_op jit(solution)/shard_map/ppermute | solution.py:26
  327.7 8.8 copy-start.30
  327.7 8.8 copy-start.76
  334.8 10.4 copy-start.94
  351.4 29.1 %copy-start.1 = (bf16[512,1536]{1,0:T(8,128)(2,1)}, bf16[512,1536]{1,0:T(8,128)(2,1)S(1)}, u32[]{:S(2)}) copy-start(bf16[512,1536]{1,0:T(8,128)(2,1)S(1)} %get-tuple-element.2333) | copy-start | bytes 4718596
  366.5 52.9 %collective-permute-start.2 = (bf16[1,24,64,64]{3,2,1,0:T(8,128)(2,1)}, bf16[1,24,64,64]{3,2,1,0:T(8,128)(2,1)}, u32[]{:S(2)}, u32[]{:S(2)}) collective-permute-start(bf16[1,24,64,64]{3,2,1,0:T(8,128)(2,1)} %fusion.230), channel_id=1, source_target_pairs={{0,16},{16,0},{1,17},{17,1},{2,18},{18,2},{3,19},{19,3},{4,20},{20... | collective-permute-start | bytes 589832 | tf_op jit(solution)/shard_map/ppermute | solution.py:26
  396.4 13.4 %copy-start.17 = (f32[512,1536]{1,0:T(8,128)S(1)}, f32[512,1536]{1,0:T(8,128)}, u32[]{:S(2)}) copy-start(f32[512,1536]{1,0:T(8,128)} %reverse.3) | copy-start | bytes 9437188
  425.1 8.7 copy-start.92
  425.1 8.7 copy-start.72
  448.9 8.2 copy-start.39
  461.0 8.6 copy-start.92
  461.0 8.7 copy-start.72
  484.9 8.2 copy-start.39
  497.0 8.6 copy-start.92
  497.0 8.7 copy-start.72
  520.9 8.2 copy-start.39
  532.9 8.6 copy-start.92
  532.9 8.7 copy-start.72
  556.8 8.1 copy-start.39
  598.4 8.2 copy-start.41
  634.0 8.1 copy-start.41
  669.5 8.1 copy-start.41
  704.9 8.1 copy-start.41
  748.2 24.7 %copy-start.45 = (f32[4,128,64]{2,1,0:T(8,128)S(1)}, f32[4,128,64]{2,1,0:T(8,128)}, u32[]{:S(2)}) copy-start(f32[4,128,64]{2,1,0:T(8,128)} %copy.522) | copy-start | bytes 393220
  748.2 24.7 %copy-start.46 = (f32[512,64]{1,0:T(8,128)S(1)}, f32[512,64]{1,0:T(8,128)}, u32[]{:S(2)}) copy-start(f32[512,64]{1,0:T(8,128)} %rev.114) | copy-start | bytes 393220
  748.2 24.7 %copy-start.2 = (bf16[512,1536]{1,0:T(8,128)(2,1)S(1)}, bf16[512,1536]{1,0:T(8,128)(2,1)}, u32[]{:S(2)}) copy-start(bf16[512,1536]{1,0:T(8,128)(2,1)} %copy-done.1) | copy-start | bytes 4718596
  748.2 24.7 %copy-start.79 = (f32[1536]{0:T(1024)S(1)}, f32[1536]{0:T(1024)}, u32[]{:S(2)}) copy-start(f32[1536]{0:T(1024)} %copy-done.78) | copy-start | bytes 18436
  791.5 5.7 collective-permute-start.3
  814.2 47.7 %copy-start.98 = (f32[512]{0:T(512)S(1)}, f32[512]{0:T(512)}, u32[]{:S(2)}) copy-start(f32[512]{0:T(512)} %copy-done.97) | copy-start | bytes 6148
  814.2 47.7 %copy-start.32 = (bf16[1,512,768]{2,1,0:T(8,128)(2,1)S(1)}, bf16[1,512,768]{2,1,0:T(8,128)(2,1)}, u32[]{:S(2)}) copy-start(bf16[1,512,768]{2,1,0:T(8,128)(2,1)} %param.38) | copy-start | bytes 2359300
  1063.1 10.2 slice-start
  1063.1 8.8 copy-start.60
  1063.1 9.5 copy-start.69
  1063.1 10.2 slice-start.1
  (118 other events, 485.0 us)
Sparse Core Ops, SparseCore 0:
  10.3 57.0 all-gather.2
  69.7 41.3 all-gather.4
  805.8 257.2 all-reduce.28
where the time goes:
time: 1100 us; the launch traced here: 1080 us
  local copies, waits for them, and re-layouts  336 us (31%)
  matrix products  265 us (24%)
  waiting for transfers between devices  207 us (19%)
  other arithmetic  142 us (13%)
  blocking collectives  85.5 us (8%)
  loops' own time  24 us (2%)
  between operations  15.6 us (1%)
    psum x1, waiting for transfers between devices, body(): lax.psum((grad_norm_gain, grad_w_zx, grad_w_bc, grad_w_dt, grad_conv_w, g...  200 us
    dot_general x24, matrix products, block_step(): y_inner = jnp.einsum('hts,shp->thp', weighted, inputs_dt, precision=highest)  108 us
    unnamed x228, local copies, waits for them, and re-layouts  52.9 us
    rev x2, local copies, waits for them, and re-layouts, one_half(): jnp.flip(x_in, axis=0)  49.4 us
    dot_general x32, matrix products, block_step(): jnp.einsum('tn,hpn->thp', c_block, states, precision=highest)  48.6 us
    dot_general x24, matrix products, block_step(): jnp.einsum('shp,sn->hpn', inputs_dt * tail_weights[:, :, None], b_block,...  48.2 us
    psum x1, blocking collectives, body(): lax.psum((grad_norm_gain, grad_w_zx, grad_w_bc, grad_w_dt, grad_conv_w, g...  42.1 us
    squeeze x48, local copies, waits for them, and re-layouts, scan_dir(): final_carry, results = lax.scan(advance, initial, sliced)  41.2 us
  transfers between devices with their start and end apart: 7, of which 3 were waited for; matrix products, arithmetic and copies ran while one was open for 30% of the time, Pallas kernels for 0%

commit v1 on v0

--- a/solution.py
+++ b/solution.py
@@ -131,11 +131,34 @@
     doc_lengths,
     out_grad,
 ):
+
+    def link_point_for(vec):
+        earlier, w2, met_up = (jax.lax.axis_size("dp"), jax.lax.axis_index("dp"), vec.shape[0])
+        made = list(map(lambda k: (k, (k + 1) % earlier), range(earlier)))
+        row_list = list(map(lambda k: (k, (k - 1) % earlier), range(earlier)))
+        piece_next = jnp.zeros((*vec.shape[:0], earlier * met_up, *vec.shape[1:]), vec.dtype)
+        state_next = parts_out = vec
+        piece_next = lax.dynamic_update_slice_in_dim(piece_next, vec, w2 * met_up, axis=0)
+        to_i = 1
+        side_arr = earlier // 2
+        while to_i < side_arr + 1:
+            state_next = jax.lax.ppermute(state_next, "dp", made)
+            piece_next = lax.dynamic_update_slice_in_dim(
+                piece_next, state_next, (w2 - to_i) % earlier * met_up, axis=0
+            )
+            if to_i < earlier - side_arr:
+                parts_out = jax.lax.ppermute(parts_out, "dp", row_list)
+                piece_next = lax.dynamic_update_slice_in_dim(
+                    piece_next, parts_out, (w2 + to_i) % earlier * met_up, axis=0
+                )
+            to_i += 1
+        return piece_next
+
     direction = lax.axis_index("dir")
     forward_side = direction == 0
     full_zx, full_bc, full_dt, full_out = (
         lax.all_gather(w_zx, "dp", axis=0, tiled=True),
-        lax.all_gather(w_bc, "dp", axis=0, tiled=True),
+        link_point_for(w_bc),
         lax.all_gather(w_dt, "dp", axis=0, tiled=True),
         lax.all_gather(w_out, "dp", axis=0, tiled=True),
     )

time: 1100 us -> 1100 us (level)
  starting transfers between devices: 7 us -> 38.9 us
  blocking collectives: 85.5 us -> 60.5 us
  waiting for transfers between devices: 207 us -> 218 us
    ppermute x0 -> x15, starting transfers between devices: none -> 32.4 us  [the longest x7 31.4 us: link_point_for(): parts_out = jax.lax.ppermute(parts_out, 'dp', row_list)]
    all_gather x1 -> x0, blocking collectives: 24.4 us -> none  [body(): lax.all_gather(w_bc, 'dp', axis=0, tiled=True)]
    ppermute x0 -> x15, waiting for transfers between devices: none -> 14.5 us  [the longest x8 14.4 us: link_point_for(): state_next = jax.lax.ppermute(state_next, 'dp', made)]
    unnamed x228 -> x232, local copies, waits for them, and re-layouts: 52.9 us -> 49.2 us
  transfers between devices with their start and end apart: 7 -> 22, of which waited for: 3 -> 9; matrix products, arithmetic and copies ran while one was open for 30% -> 29% of each run, Pallas kernels for 0% -> 0%
where the time goes in v1:
time: 1100 us; the launch traced here: 1090 us
  local copies, waits for them, and re-layouts  331 us (30%)
  matrix products  260 us (24%)
  waiting for transfers between devices  218 us (20%)
  other arithmetic  143 us (13%)
  blocking collectives  60.5 us (6%)
  starting transfers between devices  38.9 us (4%)
  loops' own time  24 us (2%)
  between operations  16.1 us (1%)
    psum x1, waiting for transfers between devices, body(): lax.psum((grad_norm_gain, grad_w_zx, grad_w_bc, grad_w_dt, grad_conv_w, g...  200 us
    dot_general x24, matrix products, block_step(): y_inner = jnp.einsum('hts,shp->thp', weighted, inputs_dt, precision=highest)  108 us
    rev x2, local copies, waits for them, and re-layouts, one_half(): jnp.flip(x_in, axis=0)  49.5 us
    unnamed x232, local copies, waits for them, and re-layouts  49.2 us
    dot_general x24, matrix products, block_step(): jnp.einsum('shp,sn->hpn', inputs_dt * tail_weights[:, :, None], b_block,...  48.2 us
    dot_general x32, matrix products, block_step(): jnp.einsum('tn,hpn->thp', c_block, states, precision=highest)  45.6 us
    squeeze x48, local copies, waits for them, and re-layouts, scan_dir(): final_carry, results = lax.scan(advance, initial, sliced)  41.2 us
    psum x1, blocking collectives, body(): lax.psum((grad_norm_gain, grad_w_zx, grad_w_bc, grad_w_dt, grad_conv_w, g...  39.8 us
  transfers between devices with their start and end apart: 22, of which 9 were waited for; matrix products, arithmetic and copies ran while one was open for 29% of the time, Pallas kernels for 0%

profile of v1, /device:TPU:0, one launch (start us, length us, event | category | flops | bytes accessed | tf_op | source)
XLA Modules:
  0.0 1090.5 jit_solution(8769417071026637926)
XLA Ops:
  8.5 5.0 collective-permute-start.1
  17.7 20.8 %all_gather.9 = bf16[768,48]{1,0:T(8,128)(2,1)S(1)} all-gather(bf16[48,48]{1,0:T(8,128)(2,1)} %param.29), channel_id=1, replica_groups=mesh['dir'=2,'dp'=16] {'dp'}, dimensions={0}, use_global_device_ids=true | all-gather | bytes 78336 | tf_op jit(solution)/shard_map/all_gather | solution.py:162
  53.4 4.4 collective-permute-start.5
  59.3 4.6 collective-permute-start.7
  65.4 4.4 collective-permute-start.9
  71.2 4.4 collective-permute-start.11
  77.0 4.4 collective-permute-start.13
  82.9 5.8 collective-permute-done.14
  89.2 4.6 fusion.287
  105.2 4.9 fusion.204
  113.0 24.8 %rev.107 = f32[512,1536]{1,0:T(8,128)} reverse(f32[512,1536]{1,0:T(8,128)} %slice.328), dimensions={0} | reverse | bytes 6291456 | tf_op jit(solution)/shard_map/jvp()/while/body/eval_jaxpr/jit(_flip)/rev | solution.py:203
  137.8 5.5 reshape.1386
  143.3 5.5 reshape.1387
  148.8 6.1 copy.490
  160.0 59.0 %while.230 = (s32[]{:T(128)}, f32[24,64,64]{2,1,0:T(8,128)S(1)}, s32[]{:T(128)}, f32[4,128,24,64]{1,3,2,0:T(8,128)}, f32[4,24,64,64]{3,2,1,0:T(8,128)}, /*index=...) while((s32[]{:T(128)}, f32[24,64,64]{2,1,0:T(8,128)S(1)}, ...), condition=%wide.region_8.10_spmd.clone, body=%wide.region_6.9_spmd.clone.sunk | while | flops 620061952 | bytes 7651091 | solution.py:99
  190.9 4.3 fusion.441
  205.7 4.3 fusion.441
  219.1 6.3 copy.484
  230.3 56.7 %while.229 = (s32[]{:T(128)}, f32[24,64,64]{2,1,0:T(8,128)S(1)}, s32[]{:T(128)}, f32[4,128,24,64]{1,3,2,0:T(8,128)}, f32[4,24,64,64]{3,2,1,0:T(8,128)}, /*index=...) while((s32[]{:T(128)}, f32[24,64,64]{2,1,0:T(8,128)S(1)}, ...), condition=%wide.region_5.7_spmd.clone, body=%wide.region_3.6_spmd.clone.sunk | while | flops 620061952 | bytes 7651091 | solution.py:99
  231.4 4.3 fusion.430
  290.8 5.8 copy.544
  296.6 4.7 reshape.1381
  301.3 15.7 %rev.110 = f32[512,1536]{1,0:T(8,128)} reverse(f32[512,1536]{1,0:T(8,128)S(1)} %reshape.1381), dimensions={0} | reverse | bytes 6291456 | tf_op jit(solution)/shard_map/jvp()/while/body/eval_jaxpr/jit(_flip)/rev | solution.py:210
  317.0 5.8 copy.543
  322.9 6.3 reshape.1380
  329.2 5.2 broadcast_multiply_fusion.4
  338.0 7.1 multiply_reduce_fusion.16
  350.5 5.0 multiply_reduce_fusion.12
  356.0 5.7 multiply_reduce_fusion.13
  371.4 5.5 fusion.230
  382.0 5.0 reduce-window.64
  390.8 16.0 %reverse.3 = f32[512,1536]{1,0:T(8,128)} reverse(bf16[512,1536]{1,0:T(8,128)(2,1)S(1)} %get-tuple-element.2333), dimensions={0} | reverse | bytes 4718592 | tf_op jit(solution)/shard_map/reverse
  406.8 6.2 copy.519
  414.4 5.0 reduce-window.66
  423.6 6.1 copy.511
  435.0 143.7 %while.232 = (s32[]{:T(128)}, f32[24]{0:T(128)}, f32[24,64,64]{2,1,0:T(8,128)S(1)}, f32[4,128,24,64]{1,3,2,0:T(8,128)}, f32[4,128,64]{1,2,0:T(8,128)}, /*index=5...) while((s32[]{:T(128)}, f32[24]{0:T(128)}, ...), condition=%wide.region_40.42_spmd.clone, body=%wide.region_28.41_spmd.clone.sunk | while | flops 1408011520 | bytes 22274224 | solution.py:99
  448.7 4.8 multiply_reduce_fusion.28
  454.5 4.7 fusion.493
  484.5 4.8 multiply_reduce_fusion.28
  490.3 4.7 fusion.493
  520.3 4.8 multiply_reduce_fusion.28
  526.1 4.7 fusion.493
  556.1 4.8 multiply_reduce_fusion.28
  561.9 4.7 fusion.493
  584.5 142.4 %while.231 = (s32[]{:T(128)}, f32[24]{0:T(128)}, f32[24,64,64]{2,1,0:T(8,128)S(1)}, f32[4,128,24,64]{1,3,2,0:T(8,128)}, f32[4,128,64]{1,2,0:T(8,128)}, /*index=5...) while((s32[]{:T(128)}, f32[24]{0:T(128)}, ...), condition=%wide.region_27.29_spmd.clone, body=%wide.region_15.28_spmd.clone.sunk | while | flops 1408011520 | bytes 19111204 | solution.py:99
  598.1 4.5 multiply_reduce_fusion.25
  603.7 4.3 fusion.462
  633.7 4.5 multiply_reduce_fusion.25
  639.3 4.3 fusion.462
  669.2 4.5 multiply_reduce_fusion.25
  674.8 4.3 fusion.462
  704.8 4.5 multiply_reduce_fusion.25
  710.4 4.3 fusion.462
  735.8 5.8 copy.553
  741.6 6.3 reshape.1385
  751.9 6.2 reshape.1384
  758.1 24.7 %rev.115 = f32[512,1536]{1,0:T(8,128)} reverse(f32[512,1536]{1,0:T(8,128)} %reshape.1384), dimensions={0} | reverse | bytes 6291456 | tf_op jit(solution)/shard_map/transpose(jvp())/while/body/eval_jaxpr/jit(_flip)/rev | solution.py:203
  793.1 5.5 multiply_reduce_fusion.11
  810.0 5.6 fusion.210
  817.7 4.4 fusion.229
  822.9 5.2 fusion.211
  830.0 39.8 %all-reduce.25 = (f32[768]{0:T(1024)}, f32[4,1664]{1,0:T(4,128)}, f32[1664]{0:T(1024)}, f32[48]{0:T(128)}, f32[48]{0:T(128)}, /*index=5*/f32[24]{0:T(128)}, f32[1536]{0:T(1024)}) all-reduce(f32[768]{0:T(1024)S(1)} %get-tuple-element.2195, f32[4,1664]{1,0:T(4,128)S(1)} %pad_add_fusion.3, ...), channel_id=1, replica_groups=mesh['dir'=2,'dp'=16] {'dir','dp'}, use_global_device_ids=true, to_apply=%region_48.50 | all-reduce | flops 10744 | bytes 85952 | tf_op jit(solution)/shard_map/psum | solution.py:290
  871.1 200.1 %all-reduce.29.cloned.1.call-done = (f32[768,3072]{1,0:T(8,128)}, f32[768,128]{1,0:T(8,128)}, f32[768,48]{0,1:T(8,128)}, f32[1536,768]{1,0:T(8,128)}) async-done(((f32[768,3072]{1,0:T(8,128)}, f32[768,128]{1,0:T(8,128)}, f32[768,48]{0,1:T(8,128)}, f32[1536,768]{1,0:T(8,128)}), (f32[768,3072]{1,0:T(8,128)}, f32[768,128]{1,0:T(8,128)}, f32[768,48]{0,1:T(8,128)}, ...) | async-done | bytes 14696464 | tf_op jit(solution)/shard_map/psum | solution.py:290
  1071.2 8.8 copy.826
  (993 shorter events, 435.0 us)
Async XLA Ops:
  7.2 37.2 %copy-start.114 = (bf16[48,128]{1,0:T(8,128)(2,1)S(1)}, bf16[48,128]{1,0:T(8,128)(2,1)}, u32[]{:S(2)}) copy-start(bf16[48,128]{1,0:T(8,128)(2,1)} %param.28) | copy-start | bytes 36868
  7.2 81.5 %copy-start.17 = (bf16[1,512,768]{2,1,0:T(8,128)(2,1)S(1)}, bf16[1,512,768]{2,1,0:T(8,128)(2,1)}, u32[]{:S(2)}) copy-start(bf16[1,512,768]{2,1,0:T(8,128)(2,1)} %param.25) | copy-start | bytes 2359300
  7.2 81.5 %copy-start.68 = (f32[768]{0:T(1024)S(1)}, f32[768]{0:T(1024)}, u32[]{:S(2)}) copy-start(f32[768]{0:T(1024)} %param.26) | copy-start | bytes 9220
  7.2 82.0 %all-gather.3.cloned.1.call-start = ((), (), s32[]{:S(2)}) async-start(), calls=%async_computation | async-start | bytes 5013504 | tf_op jit(solution)/shard_map/all_gather | solution.py:160
  7.9 342.5 %all-gather.5.cloned.1.call-start = ((), (), s32[]{:S(2)}) async-start(), calls=%async_computation.1 | async-start | bytes 2506752 | tf_op jit(solution)/shard_map/all_gather | solution.py:163
  8.0 39.2 %collective-permute-start = (bf16[48,128]{1,0:T(8,128)(2,1)}, bf16[48,128]{1,0:T(8,128)(2,1)S(1)}, u32[]{:S(2)}, u32[]{:S(2)}) collective-permute-start(bf16[48,128]{1,0:T(8,128)(2,1)} %param.28), channel_id=1, source_target_pairs={{0,1},{1,2},{2,3},{3,4},{4,5},{5,6},{6,7},{7,8},{8,9},{9,10},{10,1... | collective-permute-start | bytes 36872 | tf_op jit(solution)/shard_map/ppermute | solution.py:145
  8.5 39.1 %collective-permute-start.1 = (bf16[48,128]{1,0:T(8,128)(2,1)}, bf16[48,128]{1,0:T(8,128)(2,1)S(1)}, u32[]{:S(2)}, u32[]{:S(2)}) collective-permute-start(bf16[48,128]{1,0:T(8,128)(2,1)} %param.28), channel_id=1, source_target_pairs={{0,15},{1,0},{2,1},{3,2},{4,3},{5,4},{6,5},{7,6},{8,7},{9,8},{10,9... | collective-permute-start | bytes 36872 | tf_op jit(solution)/shard_map/ppermute | solution.py:150
  13.6 1057.6 %all-reduce.29.cloned.1.call-start = ((), (), s32[]{:S(2)}) async-start(), calls=%async_computation.2 | async-start | bytes 29392896 | tf_op jit(solution)/shard_map/psum | solution.py:290
  15.0 78.8 %copy-start.72 = (f32[512]{0:T(512)}, f32[512]{0:T(512)S(1)}, u32[]{:S(2)}) copy-start(f32[512]{0:T(512)S(1)} %fusion.272) | copy-start | bytes 6148
  16.7 88.5 %copy-start.108 = (pred[515]{0:T(1024)(128)(4,1)}, pred[515]{0:T(1024)(128)(4,1)S(1)}, u32[]{:S(2)}) copy-start(pred[515]{0:T(1024)(128)(4,1)S(1)} %get-tuple-element.2392) | copy-start | bytes 1549
  16.7 88.5 %copy-start.110 = (pred[515]{0:T(1024)(128)(4,1)}, pred[515]{0:T(1024)(128)(4,1)S(1)}, u32[]{:S(2)}) copy-start(pred[515]{0:T(1024)(128)(4,1)S(1)} %get-tuple-element.2393) | copy-start | bytes 1549
  16.7 88.5 %copy-start.112 = (pred[515]{0:T(1024)(128)(4,1)}, pred[515]{0:T(1024)(128)(4,1)S(1)}, u32[]{:S(2)}) copy-start(pred[515]{0:T(1024)(128)(4,1)S(1)} %get-tuple-element.2394) | copy-start | bytes 1549
  17.7 87.5 %copy-start.83 = (f32[1664]{0:T(1024)}, f32[1664]{0:T(1024)S(1)}, u32[]{:S(2)}) copy-start(f32[1664]{0:T(1024)S(1)} %get-tuple-element.2197) | copy-start | bytes 19972
  17.7 87.5 %copy-start.85 = (f32[1664]{0:T(1024)}, f32[1664]{0:T(1024)S(1)}, u32[]{:S(2)}) copy-start(f32[1664]{0:T(1024)S(1)} %get-tuple-element.2198) | copy-start | bytes 19972
  17.7 87.5 %copy-start.87 = (f32[1664]{0:T(1024)}, f32[1664]{0:T(1024)S(1)}, u32[]{:S(2)}) copy-start(f32[1664]{0:T(1024)S(1)} %get-tuple-element.2199) | copy-start | bytes 19972
  17.7 87.5 %copy-start.89 = (f32[1664]{0:T(1024)}, f32[1664]{0:T(1024)S(1)}, u32[]{:S(2)}) copy-start(f32[1664]{0:T(1024)S(1)} %get-tuple-element.2200) | copy-start | bytes 19972
  42.5 58.2 %copy-start.59 = (f32[512,24]{0,1:T(8,128)}, f32[512,24]{0,1:T(8,128)S(1)}, u32[]{:S(2)}) copy-start(f32[512,24]{0,1:T(8,128)S(1)} %get-tuple-element.2343) | copy-start | bytes 147460
  42.5 58.7 %copy-start.55 = (f32[512,24]{0,1:T(8,128)}, f32[512,24]{0,1:T(8,128)S(1)}, u32[]{:S(2)}) copy-start(f32[512,24]{0,1:T(8,128)S(1)} %get-tuple-element.2387) | copy-start | bytes 147460
  47.2 6.1 collective-permute-start.2
  47.6 5.8 collective-permute-start.3
  53.4 5.9 collective-permute-start.4
  53.4 5.9 collective-permute-start.5
  59.3 6.0 collective-permute-start.6
  59.3 6.0 collective-permute-start.7
  65.4 5.8 collective-permute-start.8
  65.4 5.8 collective-permute-start.9
  71.2 5.8 collective-permute-start.10
  71.2 5.8 collective-permute-start.11
  77.0 5.8 collective-permute-start.12
  77.0 5.8 collective-permute-start.13
  82.8 5.9 collective-permute-start.14
  89.1 14.9 %copy-start.45 = (bf16[512,128]{1,0:T(8,128)(2,1)}, bf16[512,128]{1,0:T(8,128)(2,1)S(1)}, u32[]{:S(2)}) copy-start(bf16[512,128]{1,0:T(8,128)(2,1)S(1)} %convolution_convert_fusion.1) | copy-start | bytes 393220
  96.8 7.2 collective-permute-start.15
  101.7 186.2 %copy-start.57 = (f32[512,24]{0,1:T(8,128)}, f32[512,24]{0,1:T(8,128)S(1)}, u32[]{:S(2)}) copy-start(f32[512,24]{0,1:T(8,128)S(1)} %rev.112) | copy-start | bytes 147460
  101.8 236.1 %copy-start.81 = (f32[1536]{0:T(1024)}, f32[1536]{0:T(1024)S(1)}, u32[]{:S(2)}) copy-start(f32[1536]{0:T(1024)S(1)} %mul.1352) | copy-start | bytes 18436
  113.0 41.9 %copy-start.39 = (f32[512,64]{1,0:T(8,128)}, f32[512,64]{1,0:T(8,128)S(1)}, u32[]{:S(2)}) copy-start(f32[512,64]{1,0:T(8,128)S(1)} %get-tuple-element.2379) | copy-start | bytes 393220
  113.0 42.1 %copy-start.37 = (f32[512,64]{1,0:T(8,128)}, f32[512,64]{1,0:T(8,128)S(1)}, u32[]{:S(2)}) copy-start(f32[512,64]{1,0:T(8,128)S(1)} %get-tuple-element.2378) | copy-start | bytes 393220
  287.9 41.3 %collective-permute-start.16 = (bf16[1,24,64,64]{3,2,1,0:T(8,128)(2,1)}, bf16[1,24,64,64]{3,2,1,0:T(8,128)(2,1)}, u32[]{:S(2)}, u32[]{:S(2)}) collective-permute-start(bf16[1,24,64,64]{3,2,1,0:T(8,128)(2,1)} %fusion.246), channel_id=1, source_target_pairs={{0,16},{16,0},{1,17},{17,1},{2,18},{18,2},{3,19},{19,3},{4,20},{20... | collective-permute-start | bytes 589832 | tf_op jit(solution)/shard_map/ppermute | solution.py:26
  338.0 8.8 copy-start.30
  338.0 8.8 copy-start.79
  345.1 10.4 copy-start.97
  361.7 29.1 %copy-start.1 = (bf16[512,1536]{1,0:T(8,128)(2,1)}, bf16[512,1536]{1,0:T(8,128)(2,1)S(1)}, u32[]{:S(2)}) copy-start(bf16[512,1536]{1,0:T(8,128)(2,1)S(1)} %get-tuple-element.2333) | copy-start | bytes 4718596
  376.8 52.9 %collective-permute-start.17 = (bf16[1,24,64,64]{3,2,1,0:T(8,128)(2,1)}, bf16[1,24,64,64]{3,2,1,0:T(8,128)(2,1)}, u32[]{:S(2)}, u32[]{:S(2)}) collective-permute-start(bf16[1,24,64,64]{3,2,1,0:T(8,128)(2,1)} %fusion.230), channel_id=1, source_target_pairs={{0,16},{16,0},{1,17},{17,1},{2,18},{18,2},{3,19},{19,3},{4,20},{20... | collective-permute-start | bytes 589832 | tf_op jit(solution)/shard_map/ppermute | solution.py:26
  406.8 13.4 %copy-start.20 = (f32[512,1536]{1,0:T(8,128)S(1)}, f32[512,1536]{1,0:T(8,128)}, u32[]{:S(2)}) copy-start(f32[512,1536]{1,0:T(8,128)} %reverse.3) | copy-start | bytes 9437188
  435.4 8.6 copy-start.95
  435.4 8.7 copy-start.75
  459.2 8.2 copy-start.42
  471.2 8.6 copy-start.95
  471.2 8.7 copy-start.75
  507.0 8.6 copy-start.95
  507.0 8.7 copy-start.75
  542.8 8.6 copy-start.95
  542.8 8.7 copy-start.75
  758.1 24.7 %copy-start.48 = (f32[4,128,64]{2,1,0:T(8,128)S(1)}, f32[4,128,64]{2,1,0:T(8,128)}, u32[]{:S(2)}) copy-start(f32[4,128,64]{2,1,0:T(8,128)} %copy.522) | copy-start | bytes 393220
  758.1 24.7 %copy-start.49 = (f32[512,64]{1,0:T(8,128)S(1)}, f32[512,64]{1,0:T(8,128)}, u32[]{:S(2)}) copy-start(f32[512,64]{1,0:T(8,128)} %rev.114) | copy-start | bytes 393220
  758.1 24.7 %copy-start.2 = (bf16[512,1536]{1,0:T(8,128)(2,1)S(1)}, bf16[512,1536]{1,0:T(8,128)(2,1)}, u32[]{:S(2)}) copy-start(bf16[512,1536]{1,0:T(8,128)(2,1)} %copy-done.1) | copy-start | bytes 4718596
  758.1 24.7 %copy-start.82 = (f32[1536]{0:T(1024)S(1)}, f32[1536]{0:T(1024)}, u32[]{:S(2)}) copy-start(f32[1536]{0:T(1024)} %copy-done.81) | copy-start | bytes 18436
  801.4 5.7 collective-permute-start.18
  828.1 41.6 %copy-start.101 = (f32[512]{0:T(512)S(1)}, f32[512]{0:T(512)}, u32[]{:S(2)}) copy-start(f32[512]{0:T(512)} %copy-done.100) | copy-start | bytes 6148
  828.1 41.6 %copy-start.32 = (bf16[1,512,768]{2,1,0:T(8,128)(2,1)S(1)}, bf16[1,512,768]{2,1,0:T(8,128)(2,1)}, u32[]{:S(2)}) copy-start(bf16[1,512,768]{2,1,0:T(8,128)(2,1)} %param.38) | copy-start | bytes 2359300
  1071.2 10.2 slice-start
  1071.2 8.8 copy-start.63
  1071.2 9.5 copy-start.74
  1071.2 10.2 slice-start.1
  (135 other events, 589.0 us)
Sparse Core Ops, SparseCore 0:
  10.3 57.2 all-gather.2
  69.9 40.8 all-gather.4
  815.7 255.4 all-reduce.28
